TPU v7x, 256 devices: a whole 4x4x8 slice. The times are simulated.
256 devices in a mesh: tile: 16 (over z, core), offs: 16 (over x, y).
Axes of the slice: x: 4, y: 4, z: 8, core: 2. Of those that a mesh axis runs over, the one named last changes fastest.
Arguments:
- traces: float32 [16, 128, 2, 2000], P('offs', 'tile'), may hold values from -6 to 6
- src_node: int32 [16, 128], P('offs', 'tile'), may hold values from 0 to 31
- rec_node: int32 [16, 128, 2], P('offs', 'tile'), may hold values from 0 to 31
- aperture: int32 [16, 128, 2], P('offs', 'tile'), may hold values from 0 to 15, all different within a row; in each aligned block of 8 rows (0 to 7, 8 to 15, ..., all dimensions but the last counted through in order) at most 2 rows name the same one
- time_table: int32 [32, 16, 2048], P(None, 'tile'), may hold values from 0 to 999
- amp_table: float32 [32, 16, 2048], P(None, 'tile'), may hold values from 0.05 to 0.5
- width_table: int32 [32, 16, 2048], P(None, 'tile'), may hold values from 0 to 2
Outputs:
- gathers: float32 [16, 16, 16, 128], P('tile', 'offs')
Inputs may be any that keep to these rules, and one draw needn't show every extreme that they name: `aperture`: each row names 2 different image tiles. Among the 8 rows of one device (aligned blocks of rows in the order offset class, block), no tile is named more than 2 times, a bound that some block reaches.
All inputs are finite; a program needn't handle non-finite values.
Results may differ from a plain program's by a relative error of at most 0.0003.
Values sent between devices are 32-bit elements; how exact they have to be, the bound alone decides.
A program may use at most 64 MiB of HBM per device.

v0:
```python
import math

import jax
import jax.numpy as jnp
from jax import lax
from jax.sharding import PartitionSpec as P

CELLS = 128
DEPTH = 16


HALF_WIDTHS = (1, 2, 4)


def triangle(signal):
    length = signal.shape[-1]
    last_axis = signal.ndim - 1
    layers = []
    for halfwidth in HALF_WIDTHS:
        padded = jnp.pad(signal, [(0, 0)] * last_axis + [(halfwidth, halfwidth)])
        summed = jnp.zeros(signal.shape, signal.dtype)
        for offset in range(-halfwidth, halfwidth + 1):
            factor = float(halfwidth + 1 - abs(offset)) / float((halfwidth + 1) ** 2)
            summed = summed + factor * lax.slice_in_dim(
                padded, halfwidth + offset, halfwidth + offset + length, axis=last_axis
            )
        layers.append(summed)
    return jnp.stack(layers, axis=-2)


def spread(filtered, sources, receivers, live, time_rows, amp_rows, width_rows):
    samples = filtered.shape[-1]
    source_time = jnp.take(time_rows, sources, axis=0)[:, None, :]
    index_time = source_time + jnp.take(time_rows, receivers, axis=0)
    width_class = jnp.maximum(
        jnp.take(width_rows, sources, axis=0)[:, None, :], jnp.take(width_rows, receivers, axis=0)
    )
    weight = (
        jnp.take(amp_rows, sources, axis=0)[:, None, :]
        * jnp.take(amp_rows, receivers, axis=0)
        * live[:, None, None]
    )
    flat = filtered.reshape(filtered.shape[0] * filtered.shape[1], -1)
    column = (width_class * samples + index_time).reshape(flat.shape[0], -1)
    picked = jnp.take_along_axis(flat, column, axis=1)
    return jnp.sum(weight.reshape(picked.shape) * picked, axis=0)


def body(traces, src_node, rec_node, aperture, time_table, amp_table, width_table):
    tiles = lax.axis_size("tile")
    blocks = traces.shape[1]
    per_block = traces.shape[2]
    samples = traces.shape[3]
    listed = aperture.shape[2]
    capacity = (3 * blocks * listed + 2 * tiles - 1) // (2 * tiles)
    slots = tiles * capacity
    targets = aperture[0].reshape(-1)
    entries = targets.shape[0]
    owner_block = jnp.arange(entries, dtype=jnp.int32) // listed
    tile_hits = (targets[:, None] == jnp.arange(tiles, dtype=jnp.int32)[None, :]).astype(jnp.int32)
    earlier = jnp.cumsum(tile_hits, axis=0) - tile_hits
    position = targets * capacity + jnp.sum(earlier * tile_hits, axis=1)
    slot_hits = (jnp.arange(slots, dtype=jnp.int32)[:, None] == position[None, :]).astype(
        jnp.float32
    )
    block_hits = (owner_block[:, None] == jnp.arange(blocks, dtype=jnp.int32)[None, :]).astype(
        jnp.float32
    )
    selector = jnp.dot(slot_hits, block_hits, precision=lax.Precision.HIGHEST)
    node_ids = (
        jnp.concatenate([src_node[0][:, None], rec_node[0]], axis=1).astype(jnp.float32) + 1.0
    )
    metadata = jnp.dot(selector, node_ids, precision=lax.Precision.HIGHEST).reshape(
        tiles, capacity, per_block + 1
    )
    filtered = triangle(traces[0])
    payload = jnp.dot(selector, filtered.reshape(blocks, -1), precision=lax.Precision.HIGHEST)
    payload = payload.reshape(tiles, capacity, per_block, 3, samples)
    arrived, arrived_meta = (
        lax.all_to_all(payload, "tile", split_axis=0, concat_axis=0, tiled=True),
        lax.all_to_all(metadata, "tile", split_axis=0, concat_axis=0, tiled=True),
    )
    received = arrived.reshape(slots, per_block, 3, samples)
    nodes_in = arrived_meta.reshape(slots, per_block + 1)
    live_flag = (nodes_in[:, 0] > 0.5).astype(jnp.int32)
    live = live_flag.astype(jnp.float32)
    sources = jnp.maximum(nodes_in[:, 0] - 1.0, 0.0).astype(jnp.int32)
    receivers = jnp.maximum(nodes_in[:, 1:] - 1.0, 0.0).astype(jnp.int32)
    time_rows = time_table[:, 0, :]
    amp_rows = amp_table[:, 0, :]
    width_rows = width_table[:, 0, :]
    points = time_rows.shape[1]
    group = math.gcd(slots, max(1, 128 // per_block))
    order = jnp.arange(slots, dtype=jnp.int32)
    rounds = slots // group

    def accumulate(index, total):
        return total + spread(
            jnp.take(received, order, axis=0),
            jnp.take(sources, order),
            jnp.take(receivers, order, axis=0),
            jnp.take(live, order),
            time_rows,
            amp_rows,
            width_rows,
        )

    image = lax.fori_loop(0, rounds, accumulate, jnp.zeros((points,), jnp.float32))
    planes = image.reshape(DEPTH, 1, CELLS)
    slab = lax.all_to_all(planes, "offs", split_axis=0, concat_axis=1, tiled=True)
    return slab[None]


def solution(mesh):
    return jax.shard_map(
        body,
        mesh=mesh,
        in_specs=(
            P("offs", "tile", None, None),
            P("offs", "tile"),
            P("offs", "tile", None),
            P("offs", "tile", None),
            P(None, "tile", None),
            P(None, "tile", None),
            P(None, "tile", None),
        ),
        out_specs=P("tile", "offs", None, None),
        check_vma=False,
    )
```

profile of v0, /device:TPU:1, one launch (start us, length us, event | category | flops | bytes accessed | tf_op | source)
XLA Modules:
  0.0 1693.6 jit_solution(8699106205035364880)
XLA Ops:
  0.0 0.8 copy.36
  1.4 1.5 fusion.23
  2.9 10.0 all-to-all-start
  13.0 4.7 add_bitcast_fusion.2
  18.2 0.4 reshape.229
  19.0 1.4 fusion.8
  20.4 2.4 copy.46
  23.3 7.2 all-to-all-start.1
  30.6 0.6 gather_fusion.2
  31.4 0.8 gather_fusion.10
  32.1 0.8 gather_fusion.8
  33.0 0.7 gather_fusion
  33.7 0.7 gather_fusion.7
  34.4 0.7 gather_fusion.9
  35.9 0.7 fusion.5
  37.0 0.4 copy-done
  37.9 0.8 gather_fusion.3
  38.6 1.1 reshape.290
  39.7 0.7 gather_fusion.4
  40.5 0.7 gather_fusion.1
  41.1 0.5 broadcast_select_fusion.4
  41.7 0.8 broadcast_select_fusion.3
  42.5 26.6 %all-to-all-done.1 = f32[16,2,2,3,2000]{4,2,3,1,0:T(2,128)} async-done(((f32[16,2,2,3,2000]{4,2,3,1,0:T(2,128)}), f32[16,2,2,3,2000]{4,2,3,1,0:T(2,128)}, u32[]{:S(2)}, u32[]{:S(2)}) %all-to-all-start.1) | async-done | bytes 1536032 | tf_op jit(solution)/shard_map/all_to_all | solution.py:80
  69.1 3.6 gather_fusion.5
  72.7 2.6 copy.47
  75.3 3.9 gather.57
  79.2 1.6 broadcast_select_fusion
  80.8 1595.9 %gather_fusion.6 = f32[131072]{0:T(1024)} fusion(f32[64,6000]{1,0:T(8,128)S(1)} %broadcast_select_fusion, s32[131072]{0:T(1024)S(1)} %bitcast.54), kind=kCustom, calls=%fused_computation.10 | custom fusion | bytes 2097152 | tf_op jit(solution)/shard_map/while/body/eval_jaxpr/jit(take_along_axis)/gather | solution.py:45
  1676.7 1.3 gather.59
  1678.1 1.9 fusion.7
  1680.0 13.0 all_to_all.19
  1693.0 0.6 copy.71
  (58 shorter events, 4.1 us)
Async XLA Ops:
  2.9 20.4 %all-to-all-start = ((f32[16,2,3]{2,1,0:T(2,128)}), f32[16,2,3]{2,1,0:T(2,128)S(1)}, u32[]{:S(2)}, u32[]{:S(2)}) async-start(f32[16,2,3]{2,1,0:T(2,128)} %bitcast.2), calls=%async_computation | async-start | bytes 32768 | tf_op jit(solution)/shard_map/all_to_all | solution.py:81
  19.0 4.0 copy-start.3
  20.4 2.7 copy-start.4
  20.4 2.8 copy-start.5
  23.3 45.8 %all-to-all-start.1 = ((f32[16,2,2,3,2000]{4,2,3,1,0:T(2,128)}), f32[16,2,2,3,2000]{4,2,3,1,0:T(2,128)}, u32[]{:S(2)}, u32[]{:S(2)}) async-start(f32[16,2,2,3,2000]{4,2,3,1,0:T(2,128)} %copy.46), calls=%async_computation.1 | async-start | bytes 3145728 | tf_op jit(solution)/shard_map/all_to_all | solution.py:80
  31.2 4.6 copy-start.6
  36.6 0.8 copy-start
  80.8 1597.2 %copy-start.1 = (s32[32,2,2048]{2,1,0:T(2,128)S(1)}, s32[32,2,2048]{2,1,0:T(2,128)}, u32[]{:S(2)}) copy-start(s32[32,2,2048]{2,1,0:T(2,128)} %copy-done) | copy-start | bytes 1572868
  80.8 1597.2 %copy-start.2 = (f32[32,2,2048]{2,1,0:T(2,128)S(1)}, f32[32,2,2048]{2,1,0:T(2,128)}, u32[]{:S(2)}) copy-start(f32[32,2,2048]{2,1,0:T(2,128)} %reshape.290) | copy-start | bytes 1572868
  80.8 1597.2 %copy-start.7 = (pred[32,2]{1,0:T(8,128)(4,1)S(1)}, pred[32,2]{1,0:T(8,128)(4,1)}, u32[]{:S(2)}) copy-start(pred[32,2]{1,0:T(8,128)(4,1)} %copy-done.6) | copy-start | bytes 196
  80.8 1597.2 %copy-start.8 = (f32[32]{0:T(128)S(1)}, f32[32]{0:T(128)}, u32[]{:S(2)}) copy-start(f32[32]{0:T(128)} %broadcast_select_fusion.4) | copy-start | bytes 388
where the time goes:
time: 1690 us
  local copies, waits for them, and re-layouts  1620 us (96%)
  waiting for transfers between devices  26.6 us (2%)
  starting transfers between devices  17.2 us (1%)
    gather x2, local copies, waits for them, and re-layouts, spread(): picked = jnp.take_along_axis(flat, column, axis=1)  1600 us
  transfers between devices with their start and end apart: 2, of which 1 were waited for; matrix products, arithmetic and copies ran while one was open for 1% of the time, Pallas kernels for 0%

commit v1 on v0

v1 whole, which is shorter than its diff:
```python
import functools

import jax
import jax.numpy as jnp
from jax import lax
from jax.experimental import pallas as pl
from jax.experimental.pallas import tpu as pltpu
from jax.sharding import PartitionSpec as P

CELLS = 128
DEPTH = 16
ROWS = 16
HALF_WIDTHS = (1, 2, 4)
CLASSES = len(HALF_WIDTHS)


def shifted(x, lane, k):
    if k > 0:
        return pltpu.roll(jnp.where(lane < k, pltpu.roll(x, ROWS - 1, 0), x), 128 - k, 1)
    return pltpu.roll(jnp.where(lane >= 128 + k, pltpu.roll(x, 1, 0), x), -k, 1)


def migrate(blocks, meta, traces, times, amps, widths, image, filtered):
    tile = lax.axis_index("tile")
    lane = lax.broadcasted_iota(jnp.int32, (ROWS, 128), 1)
    image[...] = jnp.zeros_like(image)

    def block(b, carry):
        @pl.when((meta[b, 3] == tile) | (meta[b, 4] == tile))
        def _():
            source = meta[b, 0]
            source_time, source_amp, source_width = times[source], amps[source], widths[source]
            for i in range(2):
                x = traces[b, i]
                pairs = [shifted(x, lane, k) + shifted(x, lane, -k) for k in range(1, 5)]
                for c, h in enumerate(HALF_WIDTHS):
                    total = (h + 1) * x
                    for k in range(1, h + 1):
                        total += (h + 1 - k) * pairs[k - 1]
                    filtered[i, pl.ds(c * ROWS, ROWS)] = total * (1.0 / (h + 1) ** 2)
            for i in range(2):
                receiver = meta[b, 1 + i]
                sample = source_time + times[receiver]
                weight = source_amp * amps[receiver]
                row = jnp.maximum(source_width, widths[receiver]) * ROWS + (sample >> 7)
                column = sample & 127
                for z in (0, 8):
                    picked = jnp.zeros((8, 128), jnp.float32)
                    for r in range(CLASSES * ROWS):
                        values = jnp.broadcast_to(filtered[i, pl.ds(r, 1)], (8, 128))
                        values = jnp.take_along_axis(
                            values, column[z : z + 8], axis=1, mode="promise_in_bounds"
                        )
                        picked = jnp.where(row[z : z + 8] == r, values, picked)
                    image[pl.ds(z, 8)] += weight[z : z + 8] * picked

        return carry

    lax.fori_loop(0, blocks, block, 0)


def body(traces, src_node, rec_node, aperture, time_table, amp_table, width_table):
    signal = jnp.pad(traces[0], ((0, 0), (0, 0), (0, ROWS * 128 - traces.shape[3])))
    signal = signal.reshape(signal.shape[0], signal.shape[1], ROWS, 128)
    signal = lax.all_gather(signal, "tile", axis=0, tiled=True)
    meta = jnp.concatenate([src_node[0][:, None], rec_node[0], aperture[0]], axis=1)
    meta = lax.all_gather(meta, "tile", axis=0, tiled=True)
    nodes = time_table.shape[0]
    tables = [t.reshape(nodes, DEPTH, CELLS) for t in (time_table, amp_table, width_table)]
    image = pl.pallas_call(
        functools.partial(migrate, signal.shape[0]),
        out_shape=jax.ShapeDtypeStruct((DEPTH, CELLS), jnp.float32),
        in_specs=[pl.BlockSpec(memory_space=pltpu.SMEM)]
        + [pl.BlockSpec(memory_space=pltpu.VMEM)] * 4,
        out_specs=pl.BlockSpec(memory_space=pltpu.VMEM),
        scratch_shapes=[pltpu.VMEM((2, CLASSES * ROWS, 128), jnp.float32)],
        name="migrate",
    )(meta, signal, *tables)
    planes = image.reshape(DEPTH, 1, CELLS)
    slab = lax.all_to_all(planes, "offs", split_axis=0, concat_axis=1, tiled=True)
    return slab[None]


def solution(mesh):
    return jax.shard_map(
        body,
        mesh=mesh,
        in_specs=(
            P("offs", "tile", None, None),
            P("offs", "tile"),
            P("offs", "tile", None),
            P("offs", "tile", None),
            P(None, "tile", None),
            P(None, "tile", None),
            P(None, "tile", None),
        ),
        out_specs=P("tile", "offs", None, None),
        check_vma=False,
    )
```

time: 1690 us -> 87.6 us (0.05)
  the two profiles are of different devices: /device:TPU:1 before, /device:TPU:33 now
where the time goes in v1:
time: 87.6 us; the launch traced here: 87.3 us
  blocking collectives  32.8 us (37%)
  waiting for transfers between devices  20.7 us (24%)
  Pallas kernels  15.8 us (18%)
  between operations  13.4 us (15%)
  local copies, waits for them, and re-layouts  4.56 us (5%)
    all_gather x1, waiting for transfers between devices, body(): signal = lax.all_gather(signal, 'tile', axis=0, tiled=True)  20.7 us
    all_gather x1, blocking collectives, body(): meta = lax.all_gather(meta, 'tile', axis=0, tiled=True)  19.9 us
    pallas_call x1, Pallas kernels, body(): pl.pallas_call(functools.partial(migrate, signal.shape[0]), out_shape=jax...  15.8 us
    all_to_all x1, blocking collectives, body(): lax.all_to_all(planes, 'offs', split_axis=0, concat_axis=1, tiled=True)  12.9 us
  transfers between devices with their start and end apart: 1, of which 1 were waited for; matrix products, arithmetic and copies ran while one was open for 3% of the time, Pallas kernels for 0%

profile of v1, /device:TPU:33, one launch (start us, length us, event | category | flops | bytes accessed | tf_op | source)
XLA Modules:
  0.0 87.3 jit_solution(37449096402517152)
XLA Ops:
  6.5 0.0 all-gather.2.cloned.1.call-start
  6.5 1.0 %pad.4 = f32[8,2,2048]{2,1,0:T(2,128)S(1)} pad(f32[8,2,2000]{2,1,0:T(2,128)} %bitcast.14, f32[]{:T(128)} %constant.2.clone.1), padding=0_0x0_0x0_48 | pad | bytes 259076 | tf_op jit(solution)/shard_map/jit(_pad)/pad | solution.py:63
  7.5 0.8 reshape.19
  8.3 0.0 all-gather.2.cloned.1.call-update
  8.3 0.7 copy.11
  9.0 0.8 copy.12
  9.8 0.8 copy.13
  10.5 0.1 pad_add_fusion
  10.6 19.9 %all_gather.6.meta = s32[128,5]{1,0:T(8,128)} all-gather(s32[8,5]{1,0:T(8,128)S(1)} %pad_add_fusion), channel_id=1, replica_groups=mesh['tile'=16,'offs'=16] {'tile'}, dimensions={0}, use_global_device_ids=true | all-gather | bytes 2720 | tf_op jit(solution)/shard_map/all_gather | solution.py:67
  30.5 20.7 %all-gather.2.cloned.1.call-done.traces = f32[128,2,16,128]{3,2,1,0:T(8,128)} async-done(((f32[8,2,16,128]{3,2,1,0:T(8,128)}), f32[128,2,16,128]{3,2,1,0:T(8,128)}) %all-gather.2.cloned.1.call-update) | async-done | bytes 2097168 | tf_op jit(solution)/shard_map/all_gather | solution.py:65
  51.2 15.8 %migrate.1 = f32[16,128]{1,0:T(8,128)} custom-call(s32[128,5]{1,0:T(8,128)} %all_gather.6.meta, f32[128,2,16,128]{3,2,1,0:T(8,128)} %all-gather.2.cloned.1.call-done.traces, s32[32,16,128]{2,1,0:T(8,128)} %bitcast.11, f32[32,16,128]{2,1,0:T(8,128)} %bitcast.12, s32[32,16,128]{2,1,0:T(8,128)} %bitcast.13), custom_call_target="tpu_custom_call" | custom-call | tf_op jit(solution)/shard_map/migrate/pallas_call | solution.py:70
  67.0 12.9 %all_to_all.4 = f32[16,1,128]{2,1,0:T(1,128)S(1)} all-to-all(f32[16,1,128]{2,1,0:T(1,128)} %bitcast.15), channel_id=1, replica_groups=mesh['tile'=16,'offs'=16] {'offs'}, dimensions={0} | all-to-all | bytes 16384 | tf_op jit(solution)/shard_map/all_to_all | solution.py:80
  79.9 0.6 copy.16
Async XLA Ops:
  6.5 44.7 %all-gather.2.cloned.1.call-start = ((), (), s32[]{:S(2)}) async-start(), calls=%async_computation.1 | async-start | bytes 2228224 | tf_op jit(solution)/shard_map/all_gather | solution.py:65
Sparse Core Ops, SparseCore 0:
  9.2 41.9 all-gather.1

commit v2 on v1

v2 whole, which is shorter than its diff:
```python
import jax
import jax.numpy as jnp
from jax import lax
from jax.experimental import pallas as pl
from jax.experimental.pallas import tpu as pltpu
from jax.sharding import PartitionSpec as P

CELLS = 128
DEPTH = 16
ROWS = 16
LANES = 128
SPLIT = jnp.bfloat16
HALF_WIDTHS = (1, 2, 4)
CLASSES = len(HALF_WIDTHS)
EDGE = 16
REACH = 4
MESH = pl.DeviceIdType.MESH


def band():
    depth = LANES + EDGE
    k = lax.broadcasted_iota(jnp.int32, (depth, CLASSES * LANES), 0)
    column = lax.broadcasted_iota(jnp.int32, (depth, CLASSES * LANES), 1)
    far = jnp.where(k < LANES + 2 * REACH, k - LANES - 2 * REACH, 4 * LANES)
    place = jnp.where(k < LANES + REACH, k, far)
    apart = jnp.abs(place - (column & (LANES - 1)))
    top = jnp.where(column < LANES, HALF_WIDTHS[0] + 1, HALF_WIDTHS[1] + 1)
    top = jnp.where(column < 2 * LANES, top, HALF_WIDTHS[2] + 1)
    return jnp.maximum(top - apart, 0).astype(jnp.float32).astype(SPLIT)


def halves(x):
    high = x.astype(SPLIT)
    return high, (x - high.astype(jnp.float32)).astype(SPLIT)


def migrate(
    traces, src, rec, aper, time_hbm, amp_hbm, width_hbm, out,
    raw, own, send, recv, note, notes, notes_s, src_s, rec_s, aper_s,
    times, amps, widths, weights, filtered, image,
    local, send_sem, recv_sem, note_send, note_recv, row_send, row_recv,
):
    me = lax.axis_index("tile")
    column = lax.axis_index("offs")
    tiles = recv.shape[0]
    classes = out.shape[0]
    blocks, pair = own.shape[0], own.shape[1]
    samples = raw.shape[2]
    loads = [
        pltpu.make_async_copy(a, b, local.at[i])
        for i, (a, b) in enumerate(
            (
                (aper.at[0], aper_s),
                (src, src_s),
                (rec.at[0], rec_s),
                (traces.at[0], raw),
                (time_hbm, times),
                (amp_hbm, amps),
                (width_hbm, widths),
            )
        )
    ]
    barrier = pltpu.get_barrier_semaphore()
    for load in loads:
        load.start()

    def greet_tile(k, carry):
        pl.semaphore_signal(
            barrier, inc=1, device_id={"tile": lax.rem(me + k, tiles)}, device_id_type=MESH
        )
        return carry

    def greet_offs(k, carry):
        pl.semaphore_signal(
            barrier, inc=1, device_id={"offs": lax.rem(column + k, classes)}, device_id_type=MESH
        )
        return carry

    lax.fori_loop(1, tiles, greet_tile, 0)
    lax.fori_loop(1, classes, greet_offs, 0)

    weights[...] = band()
    image[...] = jnp.zeros_like(image)
    own[:, :, pl.ds(ROWS - 8, 8), :] = jnp.zeros((blocks, pair, 8, LANES), jnp.float32)
    for load in loads[:4]:
        load.wait()

    def lay(b, carry):
        for c in range(samples // LANES):
            own[b, :, c, :] = raw[b, :, pl.ds(c * LANES, LANES)]
        rest = samples % LANES
        if rest:
            own[b, :, samples // LANES, pl.ds(0, rest)] = raw[b, :, pl.ds(samples - rest, rest)]
        return carry

    lax.fori_loop(0, blocks, lay, 0)
    lane = lax.broadcasted_iota(jnp.int32, (1, LANES), 1)

    def pack(k, carry):
        peer = lax.rem(me + k, tiles)
        first, second, named = jnp.int32(0), jnp.int32(0), jnp.int32(0)
        for b in range(blocks):
            hit = (aper_s[0, b] == peer) | (aper_s[1, b] == peer)
            first = jnp.where(hit & (named == 0), b, first)
            second = jnp.where(hit & (named == 1), b, second)
            named = named + hit.astype(jnp.int32)
        line = jnp.zeros((1, LANES), jnp.int32)
        for s, b in enumerate((first, second)):
            send[k, s] = own[b]
            line = jnp.where(lane == 4 * s, (named > s).astype(jnp.int32), line)
            line = jnp.where(lane == 4 * s + 1, src_s[0, b], line)
            line = jnp.where(lane == 4 * s + 2, rec_s[0, b], line)
            line = jnp.where(lane == 4 * s + 3, rec_s[1, b], line)
        note[pl.ds(k, 1)] = line
        return carry

    lax.fori_loop(0, tiles, pack, 0)
    notes[pl.ds(0, 1)] = note[pl.ds(0, 1)]
    recv[0] = send[0]

    def note_copy(k):
        return pltpu.make_async_remote_copy(
            note.at[pl.ds(k, 1)], notes.at[pl.ds(k, 1)], note_send.at[k], note_recv.at[k],
            device_id={"tile": lax.rem(me + k, tiles)}, device_id_type=MESH,
        )

    def trace_copy(k):
        return pltpu.make_async_remote_copy(
            send.at[k], recv.at[k], send_sem.at[k], recv_sem.at[k],
            device_id={"tile": lax.rem(me + k, tiles)}, device_id_type=MESH,
        )

    def each(first, last, action):
        def step(k, carry):
            action(k)
            return carry

        lax.fori_loop(first, last, step, 0)

    pl.semaphore_wait(barrier, tiles + classes - 2)
    each(1, tiles, lambda k: note_copy(k).start())
    each(1, tiles, lambda k: trace_copy(k).start())
    for load in loads[4:]:
        load.wait()
    each(1, tiles, lambda k: note_copy(k).wait_recv())
    to_scalar = pltpu.make_async_copy(notes, notes_s, local.at[len(loads)])
    to_scalar.start()
    to_scalar.wait()
    wide = lax.broadcasted_iota(jnp.int32, (ROWS, LANES), 1)

    def source(k):
        parts = []
        for s in range(2):
            for i in range(pair):
                x = recv[k, s, i]
                edge = jnp.where(
                    wide < REACH,
                    pltpu.roll(x, ROWS - 1, 0),
                    pltpu.roll(pltpu.roll(x, 1, 0), 2 * REACH, 1),
                )[:, :EDGE]
                xs, es = halves(x), halves(edge)
                parts += [jnp.concatenate([a, b], 1) for a, b in zip(xs, es)]
        total = jnp.dot(
            jnp.concatenate(parts, 0), weights[...], preferred_element_type=jnp.float32
        )
        for n in range(2 * pair):
            for c, h in enumerate(HALF_WIDTHS):
                lanes = slice(c * LANES, (c + 1) * LANES)
                high = total[2 * n * ROWS : (2 * n + 1) * ROWS, lanes]
                low = total[(2 * n + 1) * ROWS : (2 * n + 2) * ROWS, lanes]
                filtered[n, pl.ds(c * ROWS, ROWS)] = (high + low) * (1.0 / (h + 1) ** 2)
        sums = [jnp.zeros((8, LANES), jnp.float32) for _ in range(DEPTH // 8)]
        for s in range(2):
            live = notes_s[k, 4 * s] > 0
            node = notes_s[k, 4 * s + 1]
            source_time, source_amp, source_width = times[node], amps[node], widths[node]
            for i in range(pair):
                node = notes_s[k, 4 * s + 2 + i]
                sample = source_time + times[node]
                weight = jnp.where(live, source_amp * amps[node], 0.0)
                row = jnp.maximum(source_width, widths[node]) * ROWS + (sample >> 7)
                place = sample & (LANES - 1)
                for z in range(DEPTH // 8):
                    cut = slice(8 * z, 8 * z + 8)
                    picked = jnp.zeros((8, LANES), jnp.float32)
                    for r in range(CLASSES * ROWS):
                        values = jnp.broadcast_to(filtered[2 * s + i, pl.ds(r, 1)], (8, LANES))
                        values = jnp.take_along_axis(
                            values, place[cut], axis=1, mode="promise_in_bounds"
                        )
                        picked = jnp.where(row[cut] == r, values, picked)
                    sums[z] += weight[cut] * picked
        image[...] += jnp.concatenate(sums, 0)

    source(jnp.int32(0))

    def arrive(k, carry):
        trace_copy(k).wait_recv()
        source(k)
        return carry

    lax.fori_loop(1, tiles, arrive, 0)

    def row_copy(k):
        to = lax.rem(column + k, classes)
        return pltpu.make_async_remote_copy(
            image.at[pl.ds(to, 1)], out.at[pl.ds(column, 1)], row_send.at[k], row_recv.at[k],
            device_id={"offs": to}, device_id_type=MESH,
        )

    each(1, classes, lambda k: row_copy(k).start())
    out[pl.ds(column, 1)] = image[pl.ds(column, 1)]
    each(1, tiles, lambda k: note_copy(k).wait_send())
    each(1, tiles, lambda k: trace_copy(k).wait_send())
    each(1, classes, lambda k: row_copy(k).wait_send())
    each(1, classes, lambda k: row_copy(k).wait_recv())


def body(traces, src_node, rec_node, aperture, time_table, amp_table, width_table):
    tiles = lax.axis_size("tile")
    classes = lax.axis_size("offs")
    _, blocks, pair, samples = traces.shape
    nodes = time_table.shape[0]
    tables = [t.reshape(nodes, DEPTH, CELLS) for t in (time_table, amp_table, width_table)]
    f32, i32 = jnp.float32, jnp.int32
    dma = pltpu.SemaphoreType.DMA
    slab = pl.pallas_call(
        migrate,
        out_shape=jax.ShapeDtypeStruct((classes, CELLS), f32),
        in_specs=[pl.BlockSpec(memory_space=pl.ANY)] * 7,
        out_specs=pl.BlockSpec(memory_space=pltpu.VMEM),
        scratch_shapes=[
            pltpu.VMEM((blocks, pair, samples), f32),
            pltpu.VMEM((blocks, pair, ROWS, LANES), f32),
            pltpu.VMEM((tiles, 2, pair, ROWS, LANES), f32),
            pltpu.VMEM((tiles, 2, pair, ROWS, LANES), f32),
            pltpu.VMEM((tiles, LANES), i32),
            pltpu.VMEM((tiles, LANES), i32),
            pltpu.SMEM((tiles, LANES), i32),
            pltpu.SMEM((1, blocks), i32),
            pltpu.SMEM((pair, blocks), i32),
            pltpu.SMEM((2, blocks), i32),
            pltpu.VMEM((nodes, DEPTH, CELLS), i32),
            pltpu.VMEM((nodes, DEPTH, CELLS), f32),
            pltpu.VMEM((nodes, DEPTH, CELLS), i32),
            pltpu.VMEM((LANES + EDGE, CLASSES * LANES), SPLIT),
            pltpu.VMEM((2 * pair, CLASSES * ROWS, LANES), f32),
            pltpu.VMEM((DEPTH, CELLS), f32),
            dma((8,)),
            dma((tiles,)),
            dma((tiles,)),
            dma((tiles,)),
            dma((tiles,)),
            dma((classes,)),
            dma((classes,)),
        ],
        compiler_params=pltpu.CompilerParams(collective_id=0, has_side_effects=True),
        name="migrate",
    )(traces, src_node, jnp.swapaxes(rec_node, 1, 2), jnp.swapaxes(aperture, 1, 2), *tables)
    return slab[None, None]


def solution(mesh):
    return jax.shard_map(
        body,
        mesh=mesh,
        in_specs=(
            P("offs", "tile", None, None),
            P("offs", "tile"),
            P("offs", "tile", None),
            P("offs", "tile", None),
            P(None, "tile", None),
            P(None, "tile", None),
            P(None, "tile", None),
        ),
        out_specs=P("tile", "offs", None, None),
        check_vma=False,
    )
```

time: 87.6 us -> 37 us (0.42)
  the two profiles are of different devices: /device:TPU:33 before, /device:TPU:1 now
where the time goes in v2:
time: 37 us; the launch traced here: 36.8 us
  Pallas kernels  35.5 us (96%)
  local copies, waits for them, and re-layouts  1.3 us (4%)
    pallas_call x1, Pallas kernels, body(): pl.pallas_call(migrate, out_shape=jax.ShapeDtypeStruct((classes, CELLS),...  35.5 us
    unnamed x1, local copies, waits for them, and re-layouts  1.3 us

profile of v2, /device:TPU:1, one launch (start us, length us, event | category | flops | bytes accessed | tf_op | source)
XLA Modules:
  0.0 36.8 jit_solution(4783042610428140323)
XLA Ops:
  0.0 35.5 %migrate.1 = f32[16,128]{1,0:T(8,128)} custom-call(f32[1,8,2,2000]{3,2,1,0:T(2,128)} %traces.1, s32[1,8]{1,0:T(1,128)} %src.1, s32[1,2,8]{2,1,0:T(2,128)} %bitcast.10, s32[1,2,8]{2,1,0:T(2,128)} %bitcast.11, s32[32,16,128]{2,1,0:T(8,128)} %bitcast.6, f32[32,16,128]{2,1,0:T(8,128)} %bitcast.7, s32[32,16,128]{2,1,0:T(8,128)} %bitcast.8), custom_call_target="tpu_custom_call" | custom-call | tf_op jit(solution)/shard_map/migrate/pallas_call | solution.py:227
  35.5 1.3 %copy.9 = f32[1,1,16,128]{3,2,1,0:T(8,128)} copy(f32[1,1,16,128]{3,2,1,0:T(8,128)} %bitcast.9) | data formatting | bytes 16384

commit v3 on v2

--- a/solution.py
+++ b/solution.py
@@ -15,6 +15,7 @@
 EDGE = 16
 REACH = 4
 MESH = pl.DeviceIdType.MESH
+ORDER = (1, 2, 14, 8, 4, 12, 15, 3, 13, 6, 10, 7, 5, 11, 9)
 
 
 def band():
@@ -137,9 +138,15 @@
 
         lax.fori_loop(first, last, step, 0)
 
+    def turn(j):
+        k = jnp.int32(0)
+        for place, offset in enumerate(ORDER, 1):
+            k = jnp.where(j == place, offset, k)
+        return k
+
     pl.semaphore_wait(barrier, tiles + classes - 2)
     each(1, tiles, lambda k: note_copy(k).start())
-    each(1, tiles, lambda k: trace_copy(k).start())
+    each(1, tiles, lambda j: trace_copy(turn(j)).start())
     for load in loads[4:]:
         load.wait()
     each(1, tiles, lambda k: note_copy(k).wait_recv())
@@ -194,7 +201,8 @@
 
     source(jnp.int32(0))
 
-    def arrive(k, carry):
+    def arrive(j, carry):
+        k = turn(j)
         trace_copy(k).wait_recv()
         source(k)
         return carry

time: 37 us -> 33.7 us (0.911)
  Pallas kernels: 35.5 us -> 32.2 us
    pallas_call x1, Pallas kernels: 35.5 us -> 32.2 us  [body(): pl.pallas_call(migrate, out_shape=jax.ShapeDtypeStruct((classes, CELLS),...]
where the time goes in v3:
time: 33.7 us; the launch traced here: 33.6 us
  Pallas kernels  32.2 us (96%)
  local copies, waits for them, and re-layouts  1.3 us (4%)
    pallas_call x1, Pallas kernels, body(): pl.pallas_call(migrate, out_shape=jax.ShapeDtypeStruct((classes, CELLS),...  32.2 us
    unnamed x1, local copies, waits for them, and re-layouts  1.3 us

profile of v3, /device:TPU:1, one launch (start us, length us, event | category | flops | bytes accessed | tf_op | source)
XLA Modules:
  0.0 33.6 jit_solution(17326451697908417978)
XLA Ops:
  0.0 32.2 %migrate.1 = f32[16,128]{1,0:T(8,128)} custom-call(f32[1,8,2,2000]{3,2,1,0:T(2,128)} %traces.1, s32[1,8]{1,0:T(1,128)} %src.1, s32[1,2,8]{2,1,0:T(2,128)} %bitcast.10, s32[1,2,8]{2,1,0:T(2,128)} %bitcast.11, s32[32,16,128]{2,1,0:T(8,128)} %bitcast.6, f32[32,16,128]{2,1,0:T(8,128)} %bitcast.7, s32[32,16,128]{2,1,0:T(8,128)} %bitcast.8), custom_call_target="tpu_custom_call" | custom-call | tf_op jit(solution)/shard_map/migrate/pallas_call | solution.py:235
  32.3 1.3 %copy.9 = f32[1,1,16,128]{3,2,1,0:T(8,128)} copy(f32[1,1,16,128]{3,2,1,0:T(8,128)} %bitcast.9) | data formatting | bytes 16384

commit v4 on v3

--- a/solution.py
+++ b/solution.py
@@ -14,6 +14,7 @@
 CLASSES = len(HALF_WIDTHS)
 EDGE = 16
 REACH = 4
+GATHERED = 1
 MESH = pl.DeviceIdType.MESH
 ORDER = (1, 2, 14, 8, 4, 12, 15, 3, 13, 6, 10, 7, 5, 11, 9)
 
@@ -38,7 +39,7 @@
 def migrate(
     traces, src, rec, aper, time_hbm, amp_hbm, width_hbm, out,
     raw, own, send, recv, note, notes, notes_s, src_s, rec_s, aper_s,
-    times, amps, widths, weights, filtered, image,
+    times, amps, widths, weights, filtered, image, spread, lines, rows,
     local, send_sem, recv_sem, note_send, note_recv, row_send, row_recv,
 ):
     me = lax.axis_index("tile")
@@ -62,26 +63,20 @@
         )
     ]
     barrier = pltpu.get_barrier_semaphore()
+    for k in range(1, tiles):
+        pl.semaphore_signal(
+            barrier, inc=1, device_id={"tile": lax.rem(me + k, tiles)}, device_id_type=MESH
+        )
     for load in loads:
         load.start()
-
-    def greet_tile(k, carry):
-        pl.semaphore_signal(
-            barrier, inc=1, device_id={"tile": lax.rem(me + k, tiles)}, device_id_type=MESH
-        )
-        return carry
-
-    def greet_offs(k, carry):
+    for k in range(1, classes):
         pl.semaphore_signal(
             barrier, inc=1, device_id={"offs": lax.rem(column + k, classes)}, device_id_type=MESH
         )
-        return carry
-
-    lax.fori_loop(1, tiles, greet_tile, 0)
-    lax.fori_loop(1, classes, greet_offs, 0)
 
     weights[...] = band()
     image[...] = jnp.zeros_like(image)
+    spread[...] = jnp.zeros_like(spread)
     own[:, :, pl.ds(ROWS - 8, 8), :] = jnp.zeros((blocks, pair, 8, LANES), jnp.float32)
     for load in loads[:4]:
         load.wait()
@@ -121,7 +116,7 @@
 
     def note_copy(k):
         return pltpu.make_async_remote_copy(
-            note.at[pl.ds(k, 1)], notes.at[pl.ds(k, 1)], note_send.at[k], note_recv.at[k],
+            note.at[pl.ds(k, 1)], notes.at[pl.ds(k, 1)], note_send, note_recv,
             device_id={"tile": lax.rem(me + k, tiles)}, device_id_type=MESH,
         )
 
@@ -149,11 +144,20 @@
     each(1, tiles, lambda j: trace_copy(turn(j)).start())
     for load in loads[4:]:
         load.wait()
-    each(1, tiles, lambda k: note_copy(k).wait_recv())
+    others = pl.ds(0, tiles - 1)
+    pltpu.make_async_copy(notes.at[others], notes.at[others], note_recv).wait()
     to_scalar = pltpu.make_async_copy(notes, notes_s, local.at[len(loads)])
     to_scalar.start()
     to_scalar.wait()
+    pltpu.make_async_copy(note.at[others], note.at[others], note_send).wait()
     wide = lax.broadcasted_iota(jnp.int32, (ROWS, LANES), 1)
+    deep = lax.broadcasted_iota(jnp.int32, (ROWS, LANES), 0)
+    eight = lax.broadcasted_iota(jnp.int32, (8, LANES), 0)
+    ends = jnp.where(deep < 2 * REACH, deep - 2 * REACH, 4 * LANES)
+    ends = jnp.where(deep < REACH, deep + LANES, ends)
+    spots = [deep + ROWS * n for n in range(LANES // ROWS)] + [ends]
+    spots = [x.astype(jnp.float32).astype(SPLIT) for x in spots]
+    none = jnp.zeros((ROWS, LANES), SPLIT)
 
     def source(k):
         parts = []
@@ -168,15 +172,18 @@
                 xs, es = halves(x), halves(edge)
                 parts += [jnp.concatenate([a, b], 1) for a, b in zip(xs, es)]
         total = jnp.dot(
-            jnp.concatenate(parts, 0), weights[...], preferred_element_type=jnp.float32
-        )
-        for n in range(2 * pair):
+            jnp.concatenate(parts[: 2 * GATHERED], 0),
+            weights[...],
+            preferred_element_type=jnp.float32,
+        )
+        for n in range(GATHERED):
             for c, h in enumerate(HALF_WIDTHS):
                 lanes = slice(c * LANES, (c + 1) * LANES)
                 high = total[2 * n * ROWS : (2 * n + 1) * ROWS, lanes]
                 low = total[(2 * n + 1) * ROWS : (2 * n + 2) * ROWS, lanes]
                 filtered[n, pl.ds(c * ROWS, ROWS)] = (high + low) * (1.0 / (h + 1) ** 2)
         sums = [jnp.zeros((8, LANES), jnp.float32) for _ in range(DEPTH // 8)]
+        jobs = []
         for s in range(2):
             live = notes_s[k, 4 * s] > 0
             node = notes_s[k, 4 * s + 1]
@@ -185,18 +192,69 @@
                 node = notes_s[k, 4 * s + 2 + i]
                 sample = source_time + times[node]
                 weight = jnp.where(live, source_amp * amps[node], 0.0)
-                row = jnp.maximum(source_width, widths[node]) * ROWS + (sample >> 7)
-                place = sample & (LANES - 1)
-                for z in range(DEPTH // 8):
-                    cut = slice(8 * z, 8 * z + 8)
-                    picked = jnp.zeros((8, LANES), jnp.float32)
-                    for r in range(CLASSES * ROWS):
-                        values = jnp.broadcast_to(filtered[2 * s + i, pl.ds(r, 1)], (8, LANES))
-                        values = jnp.take_along_axis(
-                            values, place[cut], axis=1, mode="promise_in_bounds"
-                        )
-                        picked = jnp.where(row[cut] == r, values, picked)
-                    sums[z] += weight[cut] * picked
+                jobs.append((sample, weight, jnp.maximum(source_width, widths[node])))
+
+        def gather(n, z):
+            sample, weight, width = jobs[n]
+            row = width * ROWS + (sample >> 7)
+            place = sample & (LANES - 1)
+            cut = slice(8 * z, 8 * z + 8)
+            picked = jnp.zeros((8, LANES), jnp.float32)
+            for r in range(CLASSES * ROWS):
+                values = jnp.broadcast_to(filtered[n, pl.ds(r, 1)], (8, LANES))
+                values = jnp.take_along_axis(
+                    values, place[cut], axis=1, mode="promise_in_bounds"
+                )
+                picked = jnp.where(row[cut] == r, values, picked)
+            sums[z] += weight[cut] * picked
+
+        def prepare(n):
+            sample, weight, width = jobs[n]
+            tops = [h + 1 for h in HALF_WIDTHS]
+            top = jnp.where(width == 0, tops[0], jnp.where(width == 1, tops[1], tops[2]))
+            scale = jnp.where(
+                width == 0,
+                1.0 / tops[0] ** 2,
+                jnp.where(width == 1, 1.0 / tops[1] ** 2, 1.0 / tops[2] ** 2),
+            )
+            m = n - GATHERED
+            lines[m, 0] = (sample & (LANES - 1)).astype(jnp.float32)
+            lines[m, 1] = top.astype(jnp.float32)
+            lines[m, 2] = weight * scale
+            rows[m] = sample >> 7
+
+        def product(n, zs):
+            m = n - GATHERED
+            cols = []
+            for z in zs:
+                at = jnp.broadcast_to(lines[m, 0, pl.ds(z, 1)], (ROWS, LANES)).astype(SPLIT)
+                top = jnp.broadcast_to(lines[m, 1, pl.ds(z, 1)], (ROWS, LANES)).astype(SPLIT)
+                cols.append(
+                    jnp.concatenate([jnp.maximum(top - jnp.abs(x - at), none) for x in spots], 0)
+                )
+            got = jnp.dot(
+                jnp.concatenate(parts[2 * n : 2 * n + 2], 0),
+                jnp.concatenate(cols, 1),
+                preferred_element_type=jnp.float32,
+            )
+            got = got[:ROWS] + got[ROWS:]
+            for q, z in enumerate(zs):
+                lanes = slice(q * LANES, (q + 1) * LANES)
+                row = jnp.broadcast_to(rows[m, pl.ds(z, 1)], (8, LANES)) - eight
+                picked = jnp.where(row == 0, got[:8, lanes], 0.0)
+                picked = jnp.where(row == 8, got[8:, lanes], picked)
+                spread[z] += picked * jnp.broadcast_to(lines[m, 2, pl.ds(z, 1)], (8, LANES))
+
+        products = [(n, (z, z + 1)) for n in range(GATHERED, 2 * pair) for z in range(0, DEPTH, 2)]
+        gathers = [(n, z) for n in range(GATHERED) for z in range(DEPTH // 8)]
+        for n in range(GATHERED, 2 * pair):
+            prepare(n)
+        total_steps = max(len(products), len(gathers))
+        for step in range(total_steps):
+            for g in range(step * len(gathers) // total_steps, (step + 1) * len(gathers) // total_steps):
+                gather(*gathers[g])
+            for p in range(step * len(products) // total_steps, (step + 1) * len(products) // total_steps):
+                product(*products[p])
         image[...] += jnp.concatenate(sums, 0)
 
     source(jnp.int32(0))
@@ -205,23 +263,28 @@
         k = turn(j)
         trace_copy(k).wait_recv()
         source(k)
+        trace_copy(k).wait_send()
         return carry
 
     lax.fori_loop(1, tiles, arrive, 0)
+    image[...] += jnp.sum(spread[...], axis=1)
 
     def row_copy(k):
         to = lax.rem(column + k, classes)
         return pltpu.make_async_remote_copy(
-            image.at[pl.ds(to, 1)], out.at[pl.ds(column, 1)], row_send.at[k], row_recv.at[k],
+            image.at[pl.ds(to, 1)], out.at[pl.ds(column, 1)], row_send, row_recv,
             device_id={"offs": to}, device_id_type=MESH,
         )
 
     each(1, classes, lambda k: row_copy(k).start())
-    out[pl.ds(column, 1)] = image[pl.ds(column, 1)]
-    each(1, tiles, lambda k: note_copy(k).wait_send())
-    each(1, tiles, lambda k: trace_copy(k).wait_send())
-    each(1, classes, lambda k: row_copy(k).wait_send())
-    each(1, classes, lambda k: row_copy(k).wait_recv())
+    mine = pltpu.make_async_copy(
+        image.at[pl.ds(column, 1)], out.at[pl.ds(column, 1)], local.at[len(loads)]
+    )
+    mine.start()
+    mine.wait()
+    rest = pl.ds(0, classes - 1)
+    pltpu.make_async_copy(image.at[rest], image.at[rest], row_send).wait()
+    pltpu.make_async_copy(image.at[rest], image.at[rest], row_recv).wait()
 
 
 def body(traces, src_node, rec_node, aperture, time_table, amp_table, width_table):
@@ -236,7 +299,7 @@
         migrate,
         out_shape=jax.ShapeDtypeStruct((classes, CELLS), f32),
         in_specs=[pl.BlockSpec(memory_space=pl.ANY)] * 7,
-        out_specs=pl.BlockSpec(memory_space=pltpu.VMEM),
+        out_specs=pl.BlockSpec(memory_space=pl.ANY),
         scratch_shapes=[
             pltpu.VMEM((blocks, pair, samples), f32),
             pltpu.VMEM((blocks, pair, ROWS, LANES), f32),
@@ -254,13 +317,16 @@
             pltpu.VMEM((LANES + EDGE, CLASSES * LANES), SPLIT),
             pltpu.VMEM((2 * pair, CLASSES * ROWS, LANES), f32),
             pltpu.VMEM((DEPTH, CELLS), f32),
+            pltpu.VMEM((DEPTH, 8, CELLS), f32),
+            pltpu.VMEM((4, 3, DEPTH, CELLS), f32),
+            pltpu.VMEM((4, DEPTH, CELLS), i32),
             dma((8,)),
             dma((tiles,)),
             dma((tiles,)),
-            dma((tiles,)),
-            dma((tiles,)),
-            dma((classes,)),
-            dma((classes,)),
+            dma,
+            dma,
+            dma,
+            dma,
         ],
         compiler_params=pltpu.CompilerParams(collective_id=0, has_side_effects=True),
         name="migrate",

time: 33.7 us -> 30.8 us (0.914)
  Pallas kernels: 32.2 us -> 29.3 us
    pallas_call x1, Pallas kernels: 32.2 us -> 29.3 us  [body(): pl.pallas_call(migrate, out_shape=jax.ShapeDtypeStruct((classes, CELLS),...]
where the time goes in v4:
time: 30.8 us; the launch traced here: 30.6 us
  Pallas kernels  29.3 us (95%)
  local copies, waits for them, and re-layouts  1.3 us (4%)
    pallas_call x1, Pallas kernels, body(): pl.pallas_call(migrate, out_shape=jax.ShapeDtypeStruct((classes, CELLS),...  29.3 us
    unnamed x1, local copies, waits for them, and re-layouts  1.3 us

profile of v4, /device:TPU:1, one launch (start us, length us, event | category | flops | bytes accessed | tf_op | source)
XLA Modules:
  0.0 30.6 jit_solution(14850643796957223495)
XLA Ops:
  0.0 29.3 %migrate.1 = f32[16,128]{1,0:T(8,128)} custom-call(f32[1,8,2,2000]{3,2,1,0:T(2,128)} %traces.1, s32[1,8]{1,0:T(1,128)} %src.1, s32[1,2,8]{2,1,0:T(2,128)} %bitcast.10, s32[1,2,8]{2,1,0:T(2,128)} %bitcast.11, s32[32,16,128]{2,1,0:T(8,128)} %bitcast.6, f32[32,16,128]{2,1,0:T(8,128)} %bitcast.7, s32[32,16,128]{2,1,0:T(8,128)} %bitcast.8), custom_call_target="tpu_custom_call" | custom-call | tf_op jit(solution)/shard_map/migrate/pallas_call | solution.py:298
  29.3 1.3 %copy.9 = f32[1,1,16,128]{3,2,1,0:T(8,128)} copy(f32[1,1,16,128]{3,2,1,0:T(8,128)} %bitcast.9) | data formatting | bytes 16384

commit v5 on v4

--- a/solution.py
+++ b/solution.py
@@ -139,9 +139,17 @@
             k = jnp.where(j == place, offset, k)
         return k
 
+    def send_turn(j):
+        k = turn(j)
+        return jnp.where(me % 2 == 0, k, tiles - k)
+
+    def recv_turn(j):
+        k = turn(j)
+        return jnp.where((me + k) % 2 == 0, k, tiles - k)
+
     pl.semaphore_wait(barrier, tiles + classes - 2)
     each(1, tiles, lambda k: note_copy(k).start())
-    each(1, tiles, lambda j: trace_copy(turn(j)).start())
+    each(1, tiles, lambda j: trace_copy(send_turn(j)).start())
     for load in loads[4:]:
         load.wait()
     others = pl.ds(0, tiles - 1)
@@ -159,7 +167,36 @@
     spots = [x.astype(jnp.float32).astype(SPLIT) for x in spots]
     none = jnp.zeros((ROWS, LANES), SPLIT)
 
-    def source(k):
+    def source(k, ready):
+        jobs = []
+        for s in range(2):
+            live = notes_s[k, 4 * s] > 0
+            node = notes_s[k, 4 * s + 1]
+            source_time, source_amp, source_width = times[node], amps[node], widths[node]
+            for i in range(pair):
+                node = notes_s[k, 4 * s + 2 + i]
+                sample = source_time + times[node]
+                weight = jnp.where(live, source_amp * amps[node], 0.0)
+                jobs.append((sample, weight, jnp.maximum(source_width, widths[node])))
+
+        def prepare(n):
+            sample, weight, width = jobs[n]
+            tops = [h + 1 for h in HALF_WIDTHS]
+            top = jnp.where(width == 0, tops[0], jnp.where(width == 1, tops[1], tops[2]))
+            scale = jnp.where(
+                width == 0,
+                1.0 / tops[0] ** 2,
+                jnp.where(width == 1, 1.0 / tops[1] ** 2, 1.0 / tops[2] ** 2),
+            )
+            m = n - GATHERED
+            lines[m, 0] = (sample & (LANES - 1)).astype(jnp.float32)
+            lines[m, 1] = top.astype(jnp.float32)
+            lines[m, 2] = weight * scale
+            rows[m] = sample >> 7
+
+        for n in range(GATHERED, 2 * pair):
+            prepare(n)
+        ready()
         parts = []
         for s in range(2):
             for i in range(pair):
@@ -183,16 +220,6 @@
                 low = total[(2 * n + 1) * ROWS : (2 * n + 2) * ROWS, lanes]
                 filtered[n, pl.ds(c * ROWS, ROWS)] = (high + low) * (1.0 / (h + 1) ** 2)
         sums = [jnp.zeros((8, LANES), jnp.float32) for _ in range(DEPTH // 8)]
-        jobs = []
-        for s in range(2):
-            live = notes_s[k, 4 * s] > 0
-            node = notes_s[k, 4 * s + 1]
-            source_time, source_amp, source_width = times[node], amps[node], widths[node]
-            for i in range(pair):
-                node = notes_s[k, 4 * s + 2 + i]
-                sample = source_time + times[node]
-                weight = jnp.where(live, source_amp * amps[node], 0.0)
-                jobs.append((sample, weight, jnp.maximum(source_width, widths[node])))
 
         def gather(n, z):
             sample, weight, width = jobs[n]
@@ -207,21 +234,6 @@
                 )
                 picked = jnp.where(row[cut] == r, values, picked)
             sums[z] += weight[cut] * picked
-
-        def prepare(n):
-            sample, weight, width = jobs[n]
-            tops = [h + 1 for h in HALF_WIDTHS]
-            top = jnp.where(width == 0, tops[0], jnp.where(width == 1, tops[1], tops[2]))
-            scale = jnp.where(
-                width == 0,
-                1.0 / tops[0] ** 2,
-                jnp.where(width == 1, 1.0 / tops[1] ** 2, 1.0 / tops[2] ** 2),
-            )
-            m = n - GATHERED
-            lines[m, 0] = (sample & (LANES - 1)).astype(jnp.float32)
-            lines[m, 1] = top.astype(jnp.float32)
-            lines[m, 2] = weight * scale
-            rows[m] = sample >> 7
 
         def product(n, zs):
             m = n - GATHERED
@@ -247,8 +259,6 @@
 
         products = [(n, (z, z + 1)) for n in range(GATHERED, 2 * pair) for z in range(0, DEPTH, 2)]
         gathers = [(n, z) for n in range(GATHERED) for z in range(DEPTH // 8)]
-        for n in range(GATHERED, 2 * pair):
-            prepare(n)
         total_steps = max(len(products), len(gathers))
         for step in range(total_steps):
             for g in range(step * len(gathers) // total_steps, (step + 1) * len(gathers) // total_steps):
@@ -257,12 +267,11 @@
                 product(*products[p])
         image[...] += jnp.concatenate(sums, 0)
 
-    source(jnp.int32(0))
+    source(jnp.int32(0), lambda: None)
 
     def arrive(j, carry):
-        k = turn(j)
-        trace_copy(k).wait_recv()
-        source(k)
+        k = recv_turn(j)
+        source(k, trace_copy(k).wait_recv)
         trace_copy(k).wait_send()
         return carry
 
@@ -276,7 +285,8 @@
             device_id={"offs": to}, device_id_type=MESH,
         )
 
-    each(1, classes, lambda k: row_copy(k).start())
+    for k in range(1, classes):
+        row_copy(k).start()
     mine = pltpu.make_async_copy(
         image.at[pl.ds(column, 1)], out.at[pl.ds(column, 1)], local.at[len(loads)]
     )

time: 30.8 us -> 30.6 us (level)
  no operation moved by 1% of the time
where the time goes in v5:
time: 30.6 us; the launch traced here: 30.5 us
  Pallas kernels  29.2 us (95%)
  local copies, waits for them, and re-layouts  1.3 us (4%)
    pallas_call x1, Pallas kernels, body(): pl.pallas_call(migrate, out_shape=jax.ShapeDtypeStruct((classes, CELLS),...  29.2 us
    unnamed x1, local copies, waits for them, and re-layouts  1.3 us

profile of v5, /device:TPU:1, one launch (start us, length us, event | category | flops | bytes accessed | tf_op | source)
XLA Modules:
  0.0 30.5 jit_solution(5805842404616880941)
XLA Ops:
  0.0 29.2 %migrate.1 = f32[16,128]{1,0:T(8,128)} custom-call(f32[1,8,2,2000]{3,2,1,0:T(2,128)} %traces.1, s32[1,8]{1,0:T(1,128)} %src.1, s32[1,2,8]{2,1,0:T(2,128)} %bitcast.10, s32[1,2,8]{2,1,0:T(2,128)} %bitcast.11, s32[32,16,128]{2,1,0:T(8,128)} %bitcast.6, f32[32,16,128]{2,1,0:T(8,128)} %bitcast.7, s32[32,16,128]{2,1,0:T(8,128)} %bitcast.8), custom_call_target="tpu_custom_call" | custom-call | tf_op jit(solution)/shard_map/migrate/pallas_call | solution.py:308
  29.2 1.3 %copy.9 = f32[1,1,16,128]{3,2,1,0:T(8,128)} copy(f32[1,1,16,128]{3,2,1,0:T(8,128)} %bitcast.9) | data formatting | bytes 16384

commit v6 on v5

--- a/solution.py
+++ b/solution.py
@@ -272,7 +272,6 @@
     def arrive(j, carry):
         k = recv_turn(j)
         source(k, trace_copy(k).wait_recv)
-        trace_copy(k).wait_send()
         return carry
 
     lax.fori_loop(1, tiles, arrive, 0)
@@ -292,6 +291,7 @@
     )
     mine.start()
     mine.wait()
+    each(1, tiles, lambda k: trace_copy(k).wait_send())
     rest = pl.ds(0, classes - 1)
     pltpu.make_async_copy(image.at[rest], image.at[rest], row_send).wait()
     pltpu.make_async_copy(image.at[rest], image.at[rest], row_recv).wait()

time: 30.6 us -> 30.6 us (level)
  no operation moved by 1% of the time
where the time goes in v6:
time: 30.6 us; the launch traced here: 30.5 us
  Pallas kernels  29.2 us (95%)
  local copies, waits for them, and re-layouts  1.3 us (4%)
    pallas_call x1, Pallas kernels, body(): pl.pallas_call(migrate, out_shape=jax.ShapeDtypeStruct((classes, CELLS),...  29.2 us
    unnamed x1, local copies, waits for them, and re-layouts  1.3 us

profile of v6, /device:TPU:1, one launch (start us, length us, event | category | flops | bytes accessed | tf_op | source)
XLA Modules:
  0.0 30.5 jit_solution(12711774058366728942)
XLA Ops:
  0.0 29.2 %migrate.1 = f32[16,128]{1,0:T(8,128)} custom-call(f32[1,8,2,2000]{3,2,1,0:T(2,128)} %traces.1, s32[1,8]{1,0:T(1,128)} %src.1, s32[1,2,8]{2,1,0:T(2,128)} %bitcast.10, s32[1,2,8]{2,1,0:T(2,128)} %bitcast.11, s32[32,16,128]{2,1,0:T(8,128)} %bitcast.6, f32[32,16,128]{2,1,0:T(8,128)} %bitcast.7, s32[32,16,128]{2,1,0:T(8,128)} %bitcast.8), custom_call_target="tpu_custom_call" | custom-call | tf_op jit(solution)/shard_map/migrate/pallas_call | solution.py:308
  29.2 1.3 %copy.9 = f32[1,1,16,128]{3,2,1,0:T(8,128)} copy(f32[1,1,16,128]{3,2,1,0:T(8,128)} %bitcast.9) | data formatting | bytes 16384
